TPU v7x, 32 devices: a whole 2x2x4 slice. The times are simulated.
32 devices in a mesh: req: 16 (over z, y, x), mlp: 2 (over core).
Axes of the slice: x: 2, y: 2, z: 4, core: 2. Of those that a mesh axis runs over, the one named last changes fastest.
Arguments:
- queries: bfloat16 [16, 256, 1536], P('req'), may hold values from -90 to 90
- cached_key_slots: bfloat16 [16, 8192, 512], P('req', 'mlp'), may hold values from -5 to 5
- cached_value_slots: bfloat16 [16, 8192, 512], P('req', 'mlp'), may hold values from -6 to 6
- new_token_keys: bfloat16 [16, 256, 512], P('req', 'mlp'), may hold values from -5.05 to 5.05
- new_token_values: bfloat16 [16, 256, 512], P('req', 'mlp'), may hold values from -6 to 6
- cache_len: int32 [16], replicated, may hold values from 1 to 8192, 65536 in all
- placing: int32 [16], replicated, may hold values from 0 to 15, each once
- w_gate: bfloat16 [1536, 12288], P('req', 'mlp'), may hold values from -0.15625 to 0.15625
- w_up: bfloat16 [1536, 12288], P('req', 'mlp'), may hold values from -0.15625 to 0.15625
- w_down: bfloat16 [12288, 1536], P('mlp', 'req'), may hold values from -0.0546875 to 0.0546875
Outputs:
- mixed: bfloat16 [16, 256, 1536], P('req', 'mlp')
All inputs are finite; a program needn't handle non-finite values.
Results may differ from a plain program's by a relative error of at most 0.019.
Values may be sent and summed in bfloat16 or wider, within the bound.
A program may use at most 192 MiB of HBM per device.

v0:
```python
import jax
import jax.numpy as jnp
from jax import lax
from jax.sharding import PartitionSpec as P

HEAD_SIZE = 256
QUERY_HEADS = 6
KEY_VALUE_HEADS = 2
score_scale = 0.0625
negative = -1e30


def lookup(table, index):
    positions = jnp.arange(table.shape[0], dtype=jnp.int32)
    return jnp.sum(jnp.where(positions == index, table, 0))


def rms_rows(attended):
    wide = attended.astype(jnp.float32)
    return (wide * lax.rsqrt(jnp.mean(wide * wide, axis=-1, keepdims=True) + 1e-06)).astype(
        jnp.bfloat16
    )


def gathered_weights(weighted, denom_local, w_gate, w_up, w_down):
    token_inputs = weighted.shape[0]
    mlp_index = lax.axis_index("mlp")
    row_count = token_inputs // lax.axis_size("mlp")
    weighted, denom = lax.psum((weighted, denom_local), "mlp")
    attended = (
        (weighted / jnp.transpose(denom, (2, 0, 1))[..., None])
        .reshape(token_inputs, QUERY_HEADS * HEAD_SIZE)
        .astype(jnp.bfloat16)
    )
    normed = rms_rows(attended)
    own_attended = lax.dynamic_slice_in_dim(attended, mlp_index * row_count, row_count, 0)
    gate_sum = jnp.dot(
        normed,
        lax.all_gather(w_gate, "req", axis=0, tiled=True),
        preferred_element_type=jnp.float32,
    )
    upper_sum = jnp.dot(
        normed, lax.all_gather(w_up, "req", axis=0, tiled=True), preferred_element_type=jnp.float32
    )
    hidden = (jax.nn.silu(gate_sum) * upper_sum).astype(jnp.bfloat16)
    partial_down = jnp.dot(
        hidden,
        lax.all_gather(w_down, "req", axis=1, tiled=True),
        preferred_element_type=jnp.float32,
    )
    own_rows = lax.psum_scatter(
        partial_down.astype(jnp.bfloat16), "mlp", scatter_dimension=0, tiled=True
    ).astype(jnp.float32)
    residual = own_attended.astype(jnp.float32)
    return (residual + own_rows).astype(jnp.bfloat16)[None]


def body(
    queries,
    cached_key_slots,
    cached_value_slots,
    new_token_keys,
    new_token_values,
    cache_len,
    placing,
    w_gate,
    w_up,
    w_down,
):
    slot_index = lax.axis_index("req")
    mlp_index = lax.axis_index("mlp")
    mlp_count = lax.axis_size("mlp")
    token_inputs = queries.shape[1]
    request_cache = cached_key_slots.shape[1]
    request_new_tokens = new_token_keys.shape[1]
    query_group_width = QUERY_HEADS // KEY_VALUE_HEADS
    row_count = token_inputs // mlp_count
    request = lookup(placing, slot_index)
    live_len = lookup(cache_len, request)
    query_head_rows = queries[0].reshape(
        token_inputs, KEY_VALUE_HEADS, query_group_width, HEAD_SIZE
    )
    request_keys = cached_key_slots[0].reshape(request_cache, KEY_VALUE_HEADS, HEAD_SIZE)
    request_values = cached_value_slots[0].reshape(request_cache, KEY_VALUE_HEADS, HEAD_SIZE)
    new_key_rows = new_token_keys[0].reshape(request_new_tokens, KEY_VALUE_HEADS, HEAD_SIZE)
    new_value_rows = new_token_values[0].reshape(request_new_tokens, KEY_VALUE_HEADS, HEAD_SIZE)
    cache_pos = mlp_index * request_cache + jnp.arange(request_cache, dtype=jnp.int32)
    cache_live = cache_pos < live_len
    scores_old = (
        jnp.einsum(
            "ngrd,cgd->grnc", query_head_rows, request_keys, preferred_element_type=jnp.float32
        )
        * score_scale
    )
    scores_old = jnp.where(cache_live[None, None, None, :], scores_old, negative)
    fresh_pos = mlp_index * request_new_tokens + jnp.arange(request_new_tokens, dtype=jnp.int32)
    causal = fresh_pos[None, :] <= jnp.arange(token_inputs, dtype=jnp.int32)[:, None]
    scores_new = (
        jnp.einsum(
            "ngrd,mgd->grnm", query_head_rows, new_key_rows, preferred_element_type=jnp.float32
        )
        * score_scale
    )
    scores_new = jnp.where(causal[None, None], scores_new, negative)
    local_top = jnp.maximum(scores_old.max(-1), scores_new.max(-1))
    row_top = lax.pmax(local_top, "mlp")
    expo_old = jnp.exp(scores_old - row_top[..., None])
    expo_new = jnp.exp(scores_new - row_top[..., None])
    denom_local = expo_old.sum(-1) + expo_new.sum(-1)
    probs_old = expo_old.astype(jnp.bfloat16)
    probs_new = expo_new.astype(jnp.bfloat16)
    weighted = jnp.einsum(
        "grnc,cgd->ngrd", probs_old, request_values, preferred_element_type=jnp.float32
    )
    weighted = weighted + jnp.einsum(
        "grnm,mgd->ngrd", probs_new, new_value_rows, preferred_element_type=jnp.float32
    )
    if lax.axis_size("req") > 16:
        return gathered_weights(weighted, denom_local, w_gate, w_up, w_down)
    w_in = jnp.stack([w_gate, w_up])
    w_in = lax.all_to_all(w_in, "req", split_axis=2, concat_axis=1, tiled=True)
    w_in = lax.all_gather(w_in, "mlp", axis=2, tiled=True)
    w_out = lax.all_to_all(w_down, "req", split_axis=0, concat_axis=1, tiled=True)
    w_out = lax.all_gather(w_out, "mlp", axis=0, tiled=True)
    denom_rows = jnp.transpose(denom_local, (2, 0, 1))
    weighted = lax.psum_scatter(weighted, "mlp", scatter_dimension=0, tiled=True)
    denom = lax.psum_scatter(denom_rows, "mlp", scatter_dimension=0, tiled=True)
    attended = (
        (weighted / denom[..., None])
        .reshape(row_count, QUERY_HEADS * HEAD_SIZE)
        .astype(jnp.bfloat16)
    )
    normed = lax.all_gather(rms_rows(attended), "req", axis=0, tiled=True)
    gate_sum = jnp.dot(normed, w_in[0], preferred_element_type=jnp.float32)
    upper_sum = jnp.dot(normed, w_in[1], preferred_element_type=jnp.float32)
    hidden = (jax.nn.silu(gate_sum) * upper_sum).astype(jnp.bfloat16)
    partial_down = jnp.dot(hidden, w_out, preferred_element_type=jnp.float32)
    own_rows = lax.psum_scatter(
        partial_down.astype(jnp.bfloat16), "req", scatter_dimension=0, tiled=True
    ).astype(jnp.float32)
    return (attended.astype(jnp.float32) + own_rows).astype(jnp.bfloat16)[None]


def solution(mesh):
    in_specs = (
        P("req", None, None),
        P("req", "mlp", None),
        P("req", "mlp", None),
        P("req", "mlp", None),
        P("req", "mlp", None),
        P(),
        P(),
        P("req", "mlp"),
        P("req", "mlp"),
        P("mlp", "req"),
    )
    out_specs = P("req", "mlp", None)
    return jax.shard_map(body, mesh=mesh, in_specs=in_specs, out_specs=out_specs, check_vma=False)
```

profile of v0, /device:TPU:0, one launch (start us, length us, event | category | flops | bytes accessed | tf_op | source)
XLA Modules:
  0.0 450.4 jit_solution(2439042109606651874)
XLA Ops:
  6.5 1.4 copy.59
  8.0 6.9 %reshape_squeeze.15 = bf16[4096,2,256]{2,1,0:T(2,128)(2,1)} reshape(bf16[1,4096,512]{2,1,0:T(8,128)(2,1)} %param.11) | data formatting | bytes 8388608 | tf_op jit(solution)/shard_map/reshape;squeeze | solution.py:83
  15.1 0.6 fusion.20
  15.8 1.3 fusion.21
  17.0 0.6 add_compare_fusion
  17.6 12.0 %bitcast_reduce_fusion = (f32[2,3,256]{2,1,0:T(4,128)S(1)}, f32[2,4096,256,3]{2,1,3,0:T(8,128)}) fusion(pred[4096]{0:T(1024)(128)(4,1)S(1)} %add_compare_fusion, bf16[256,2,3,256]{0,3,2,1:T(8,128)(2,1)S(1)} %bitcast.63, bf16[4096,2,256,1]{2,1,0,3:T(2,128)(2,1)} %bitcast.61), kind=kOutput, calls=%fused_computation.1 | convolution fusion | flops 3240098304 | bytes 30156800 | tf_op jit(solution)/shard_map/ngrd,cgd->grnc/dot_general | solution.py:90
  29.6 0.3 fusion.25
  29.9 2.6 pmax.7
  32.5 11.5 %fusion.1 = f32[2,3,256]{2,1,0:T(4,128)S(1)} fusion(f32[2,4096,256,3]{2,1,3,0:T(8,128)} %get-tuple-element.8, f32[2,3,256]{2,1,0:T(4,128)S(1)} %pmax.7, pred[4096]{0:T(1024)(128)(4,1)S(1)} %add_compare_fusion), kind=kLoop, calls=%fused_computation.4 | loop fusion | flops 25164288 | bytes 25182208 | tf_op jit(solution)/shard_map/reduce_sum | solution.py:109
  44.0 0.1 fusion.12
  44.2 0.8 copy.94
  45.0 1.5 pad_maximum_fusion
  46.5 5.3 %copy.69 = bf16[2,96,6144]{1,0,2:T(2,128)(2,1)} copy(bf16[2,96,6144]{2,1,0:T(8,128)(2,1)S(1)} %pad_maximum_fusion) | data formatting | bytes 4718592 | tf_op jit(solution)/shard_map/stack | solution.py:120
  51.9 8.2 %all-to-all-start = ((bf16[2,96,6144]{1,0,2:T(2,128)(2,1)}), bf16[2,96,6144]{1,0,2:T(2,128)(2,1)S(1)}, u32[]{:S(2)}, u32[]{:S(2)}) async-start(bf16[2,96,6144]{1,0,2:T(2,128)(2,1)} %copy.69), calls=%async_computation.1 | async-start | bytes 6291456 | tf_op jit(solution)/shard_map/all_to_all | solution.py:121
  60.1 6.9 %reshape_squeeze.18 = bf16[4096,2,256]{2,1,0:T(2,128)(2,1)} reshape(bf16[1,4096,512]{2,1,0:T(8,128)(2,1)} %param.12) | data formatting | bytes 8388608 | tf_op jit(solution)/shard_map/reshape;squeeze | solution.py:84
  67.1 13.5 %fusion.3 = f32[2,3,256,256]{3,2,1,0:T(8,128)S(1)} fusion(f32[2,4096,256,3]{2,1,3,0:T(8,128)} %get-tuple-element.8, f32[2,3,256]{2,1,0:T(4,128)S(1)} %pmax.7, pred[4096]{0:T(1024)(128)(4,1)S(1)} %add_compare_fusion, bf16[4096,2,256,1]{2,1,0,3:T(2,128)(2,1)} %bitcast.62), kind=kOutput, calls=%fused_computation.6 | convolution fusion | flops 3246391296 | bytes 30943232 | tf_op jit(solution)/shard_map/grnc,cgd->ngrd/dot_general | solution.py:112
  80.6 1.6 add_bitcast_fusion
  82.3 38.9 %all-to-all-done = bf16[2,96,6144]{1,0,2:T(2,128)(2,1)S(1)} async-done(((bf16[2,96,6144]{1,0,2:T(2,128)(2,1)}), bf16[2,96,6144]{1,0,2:T(2,128)(2,1)S(1)}, u32[]{:S(2)}, u32[]{:S(2)}) %all-to-all-start) | async-done | bytes 2359328 | tf_op jit(solution)/shard_map/all_to_all | solution.py:121
  121.2 5.5 %copy.91 = bf16[2,96,16,384]{3,1,2,0:T(8,128)(2,1)} copy(bf16[2,96,16,384]{1,0,3,2:T(2,128)(2,1)S(1)} %bitcast.56) | data formatting | bytes 4718592 | tf_op jit(solution)/shard_map/all_to_all | solution.py:121
  126.8 1.0 reshape.52
  128.0 1.4 multiply_reduce_fusion
  129.4 0.3 copy.68
  129.7 0.8 multiply_convert_fusion.1
  130.7 44.9 %all_to_all.37 = bf16[16,384,96]{1,2,0:T(8,128)(2,1)} all-to-all(bf16[16,384,96]{1,2,0:T(8,128)(2,1)S(1)} %bitcast.60), channel_id=1, replica_groups=mesh['req'=16,'mlp'=2] {'req'}, dimensions={0} | all-to-all | bytes 2359296 | tf_op jit(solution)/shard_map/all_to_all | solution.py:123
  175.6 0.2 reduce-scatter.8.cloned.1.call-start
  175.9 96.7 %all-gather.4.cloned.1.call-done = bf16[2048,1536]{0,1:T(8,128)(2,1)} async-done(((bf16[128,1536]{0,1:T(8,128)(2,1)}), bf16[2048,1536]{0,1:T(8,128)(2,1)}) %all-gather.4.cloned.1.call-update) | async-done | bytes 6291472 | tf_op jit(solution)/shard_map/all_gather | solution.py:133
  272.6 8.3 %fusion.9 = f32[2048,768]{1,0:T(8,128)S(1)} fusion(bf16[2048,1536]{0,1:T(8,128)(2,1)} %all-gather.4.cloned.1.call-done, bf16[2,1536,768]{2,1,0:T(8,128)(2,1)} %all-gather.6.cloned.1.call-done), kind=kOutput, calls=%fused_computation.15 | convolution fusion | flops 4831838208 | bytes 14942208 | tf_op jit(solution)/shard_map/dot_general | solution.py:134
  280.9 7.6 %multiply_convert_fusion = bf16[2048,768]{1,0:T(8,128)(2,1)} fusion(f32[2048,768]{1,0:T(8,128)S(1)} %fusion.9, bf16[2048,1536]{0,1:T(8,128)(2,1)S(1)} %copy-done.6, bf16[2,1536,768]{2,1,0:T(8,128)(2,1)S(1)} %copy-done.7), kind=kOutput, calls=%fused_computation.9 | convolution fusion | flops 4841275392 | bytes 18087936 | tf_op jit(solution)/shard_map/dot_general | solution.py:135
  288.5 9.1 %convolution_convert_fusion = bf16[2048,1536]{1,0:T(8,128)(2,1)} fusion(bf16[2048,768]{1,0:T(8,128)(2,1)} %multiply_convert_fusion, bf16[768,1536]{0,1:T(8,128)(2,1)} %all-gather.8.cloned.1.call-done), kind=kOutput, calls=%fused_computation.8 | convolution fusion | flops 4834983936 | bytes 11796480 | tf_op jit(solution)/shard_map/dot_general | solution.py:137
  297.7 0.3 copy.73
  298.0 143.7 %reduce-scatter.8.cloned.1.call-done = bf16[128,1536]{1,0:T(8,128)(2,1)} async-done(((bf16[2048,1536]{1,0:T(8,128)(2,1)}), bf16[128,1536]{1,0:T(8,128)(2,1)}) %reduce-scatter.8.cloned.1.call-update) | async-done | bytes 393232 | tf_op jit(solution)/shard_map/reduce_scatter | solution.py:138
  441.7 1.8 fusion.16
  (45 shorter events, 0.7 us)
Async XLA Ops:
  6.5 120.3 %reduce-scatter.10.cloned.1.call-start = ((), (), s32[]{:S(2)}) async-start(), calls=%async_computation.10 | async-start | bytes 196608
  6.5 8.4 %copy-start.4 = (bf16[1,128,512]{2,1,0:T(8,128)(2,1)S(1)}, bf16[1,128,512]{2,1,0:T(8,128)(2,1)}, u32[]{:S(2)}) copy-start(bf16[1,128,512]{2,1,0:T(8,128)(2,1)} %param.13) | copy-start | bytes 393220
  8.0 7.1 %copy-start.8 = (s32[16]{0:T(128)S(1)}, s32[16]{0:T(128)}, u32[]{:S(2)}) copy-start(s32[16]{0:T(128)} %param.16) | copy-start | bytes 196
  8.0 7.8 %copy-start.9 = (s32[16]{0:T(128)S(1)}, s32[16]{0:T(128)}, u32[]{:S(2)}) copy-start(s32[16]{0:T(128)} %param.15) | copy-start | bytes 196
  29.8 14.2 %copy-start = (f32[2,3,256,128]{2,3,1,0:T(8,128)}, f32[2,3,256,128]{2,3,1,0:T(8,128)S(1)}, u32[]{:S(2)}) copy-start(f32[2,3,256,128]{2,3,1,0:T(8,128)S(1)} %get-tuple-element.10) | copy-start | bytes 2359300
  32.5 12.5 %copy-start.3 = (bf16[96,6144]{1,0:T(8,128)(2,1)S(1)}, bf16[96,6144]{1,0:T(8,128)(2,1)}, u32[]{:S(2)}) copy-start(bf16[96,6144]{1,0:T(8,128)(2,1)} %param.18) | copy-start | bytes 3538948
  51.9 69.4 %all-to-all-start = ((bf16[2,96,6144]{1,0,2:T(2,128)(2,1)}), bf16[2,96,6144]{1,0,2:T(2,128)(2,1)S(1)}, u32[]{:S(2)}, u32[]{:S(2)}) async-start(bf16[2,96,6144]{1,0,2:T(2,128)(2,1)} %copy.69), calls=%async_computation.1 | async-start | bytes 6291456 | tf_op jit(solution)/shard_map/all_to_all | solution.py:121
  60.1 7.0 %copy-start.5 = (bf16[1,128,512]{2,1,0:T(8,128)(2,1)S(1)}, bf16[1,128,512]{2,1,0:T(8,128)(2,1)}, u32[]{:S(2)}) copy-start(bf16[1,128,512]{2,1,0:T(8,128)(2,1)} %param.14) | copy-start | bytes 393220
  60.1 67.9 %reduce-scatter.6.cloned.1.call-start = ((), (), s32[]{:S(2)}) async-start(), calls=%async_computation.5 | async-start | bytes 2359296 | tf_op jit(solution)/shard_map/reduce_scatter | solution.py:126
  67.1 13.5 %copy-start.1 = (f32[2,3,256,128]{2,3,1,0:T(8,128)S(1)}, f32[2,3,256,128]{2,3,1,0:T(8,128)}, u32[]{:S(2)}) copy-start(f32[2,3,256,128]{2,3,1,0:T(8,128)} %copy-done) | copy-start | bytes 2359300
  82.3 93.6 %all-gather.6.cloned.1.call-start = ((), (), s32[]{:S(2)}) async-start(), calls=%async_computation.7 | async-start | bytes 7077888 | tf_op jit(solution)/shard_map/all_gather | solution.py:122
  126.7 3.8 copy-start.2
  126.8 145.9 %all-gather.4.cloned.1.call-start = ((), (), s32[]{:S(2)}) async-start(), calls=%async_computation.6 | async-start | bytes 6684672 | tf_op jit(solution)/shard_map/all_gather | solution.py:133
  130.5 158.1 %all-gather.8.cloned.1.call-start = ((), (), s32[]{:S(2)}) async-start(), calls=%async_computation.8 | async-start | bytes 3538944 | tf_op jit(solution)/shard_map/all_gather | solution.py:124
  175.6 266.1 %reduce-scatter.8.cloned.1.call-start = ((), (), s32[]{:S(2)}) async-start(), calls=%async_computation.9 | async-start | bytes 6684672 | tf_op jit(solution)/shard_map/reduce_scatter | solution.py:138
  272.6 8.3 %copy-start.6 = (bf16[2048,1536]{0,1:T(8,128)(2,1)S(1)}, bf16[2048,1536]{0,1:T(8,128)(2,1)}, u32[]{:S(2)}) copy-start(bf16[2048,1536]{0,1:T(8,128)(2,1)} %all-gather.4.cloned.1.call-done) | copy-start | bytes 18874372
  272.6 8.3 %copy-start.7 = (bf16[2,1536,768]{2,1,0:T(8,128)(2,1)S(1)}, bf16[2,1536,768]{2,1,0:T(8,128)(2,1)}, u32[]{:S(2)}) copy-start(bf16[2,1536,768]{2,1,0:T(8,128)(2,1)} %all-gather.6.cloned.1.call-done) | copy-start | bytes 14155780
Sparse Core Ops, SparseCore 0:
  45.1 10.0 reduce-scatter.9
  82.4 10.3 reduce-scatter.5
  126.9 24.3 all-gather.5
  154.2 118.3 all-gather.3
  274.1 9.0 all-gather.7
  297.8 143.8 reduce-scatter.7
where the time goes:
time: 451 us; the launch traced here: 450 us
  waiting for transfers between devices  280 us (62%)
  matrix products  52.4 us (12%)
  blocking collectives  47.6 us (11%)
  local copies, waits for them, and re-layouts  28.9 us (6%)
  other arithmetic  19.7 us (4%)
  between operations  13.7 us (3%)
  starting transfers between devices  8.58 us (2%)
    reduce_scatter x1, waiting for transfers between devices, body(): lax.psum_scatter(partial_down.astype(jnp.bfloat16), 'req', scatter_dimens...  144 us
    all_gather x1, waiting for transfers between devices, body(): normed = lax.all_gather(rms_rows(attended), 'req', axis=0, tiled=True)  96.7 us
    all_to_all x1, blocking collectives, body(): lax.all_to_all(w_down, 'req', split_axis=0, concat_axis=1, tiled=True)  44.9 us
    all_to_all x1, waiting for transfers between devices, body(): w_in = lax.all_to_all(w_in, 'req', split_axis=2, concat_axis=1, tiled=True)  38.9 us
    dot_general x1, matrix products, body(): jnp.einsum('grnc,cgd->ngrd', probs_old, request_values, preferred_element...  13.5 us
    dot_general x1, matrix products, body(): jnp.einsum('ngrd,cgd->grnc', query_head_rows, request_keys, preferred_ele...  12 us
    reduce_sum x2, other arithmetic, body(): denom_local = expo_old.sum(-1) + expo_new.sum(-1)  11.7 us
    dot_general x1, matrix products, body(): partial_down = jnp.dot(hidden, w_out, preferred_element_type=jnp.float32)  9.13 us
  transfers between devices with their start and end apart: 7, of which 3 were waited for; matrix products, arithmetic and copies ran while one was open for 12% of the time, Pallas kernels for 0%

commit v1 on v0

--- a/solution.py
+++ b/solution.py
@@ -130,7 +130,15 @@
         .reshape(row_count, QUERY_HEADS * HEAD_SIZE)
         .astype(jnp.bfloat16)
     )
-    normed = lax.all_gather(rms_rows(attended), "req", axis=0, tiled=True)
+    x = rms_rows(attended)
+    ways, here = (lax.axis_size("req"), lax.axis_index("req"))
+    normed, reach = (x, 1)
+    while reach < ways:
+        theirs = lax.ppermute(normed, "req", [(d, d ^ reach) for d in range(ways)])
+        mine_first = jnp.concatenate([normed, theirs], axis=0)
+        theirs_first = jnp.concatenate([theirs, normed], axis=0)
+        normed = jnp.where(here & reach == 0, mine_first, theirs_first)
+        reach = 2 * reach
     gate_sum = jnp.dot(normed, w_in[0], preferred_element_type=jnp.float32)
     upper_sum = jnp.dot(normed, w_in[1], preferred_element_type=jnp.float32)
     hidden = (jax.nn.silu(gate_sum) * upper_sum).astype(jnp.bfloat16)

time: 451 us -> 544 us (1.21)
  blocking collectives: 47.6 us -> 162 us
  waiting for transfers between devices: 280 us -> 212 us
  starting transfers between devices: 8.58 us -> 28.1 us
  other arithmetic: 19.7 us -> 30.8 us
  matrix products: 52.4 us -> 61.3 us
  local copies, waits for them, and re-layouts: 28.9 us -> 34.8 us
    all_to_all x1, blocking collectives: 44.9 us -> 159 us  [body(): lax.all_to_all(w_down, 'req', split_axis=0, concat_axis=1, tiled=True)]
    all_gather x1 -> x0, waiting for transfers between devices: 96.7 us -> none  [body(): normed = lax.all_gather(rms_rows(attended), 'req', axis=0, tiled=True)]
    ppermute x0 -> x4, waiting for transfers between devices: none -> 66.8 us  [body(): theirs = lax.ppermute(normed, 'req', [(d, d ^ reach) for d in range(ways)])]
    all_to_all x1, waiting for transfers between devices: 38.9 us -> 0.01 us  [body(): w_in = lax.all_to_all(w_in, 'req', split_axis=2, concat_axis=1, tiled=True)]
    ppermute x0 -> x4, starting transfers between devices: none -> 19.6 us  [body(): theirs = lax.ppermute(normed, 'req', [(d, d ^ reach) for d in range(ways)])]
    dot_general x1, matrix products: 9.13 us -> 21.2 us  [body(): partial_down = jnp.dot(hidden, w_out, preferred_element_type=jnp.float32)]
    select_n x0 -> x3, other arithmetic: none -> 9.8 us  [body(): normed = jnp.where(here & reach == 0, mine_first, theirs_first)]
    dot_general x1 -> x0, matrix products: 8.27 us -> none  [body(): gate_sum = jnp.dot(normed, w_in[0], preferred_element_type=jnp.float32)]
  transfers between devices with their start and end apart: 7 -> 10, of which waited for: 3 -> 4; matrix products, arithmetic and copies ran while one was open for 12% -> 12% of each run, Pallas kernels for 0% -> 0%
where the time goes in v1:
time: 544 us; the launch traced here: 543 us
  waiting for transfers between devices  212 us (39%)
  blocking collectives  162 us (30%)
  matrix products  61.3 us (11%)
  local copies, waits for them, and re-layouts  34.8 us (6%)
  other arithmetic  30.8 us (6%)
  starting transfers between devices  28.1 us (5%)
  between operations  13.3 us (2%)
    all_to_all x1, blocking collectives, body(): lax.all_to_all(w_down, 'req', split_axis=0, concat_axis=1, tiled=True)  159 us
    reduce_scatter x1, waiting for transfers between devices, body(): lax.psum_scatter(partial_down.astype(jnp.bfloat16), 'req', scatter_dimens...  145 us
    ppermute x4, waiting for transfers between devices, body(): theirs = lax.ppermute(normed, 'req', [(d, d ^ reach) for d in range(ways)])  66.8 us
    dot_general x1, matrix products, body(): partial_down = jnp.dot(hidden, w_out, preferred_element_type=jnp.float32)  21.2 us
    ppermute x4, starting transfers between devices, body(): theirs = lax.ppermute(normed, 'req', [(d, d ^ reach) for d in range(ways)])  19.6 us
    dot_general x1, matrix products, body(): jnp.einsum('grnc,cgd->ngrd', probs_old, request_values, preferred_element...  13.5 us
    dot_general x1, matrix products, body(): jnp.einsum('ngrd,cgd->grnc', query_head_rows, request_keys, preferred_ele...  12 us
    dot_general x1, matrix products, body(): upper_sum = jnp.dot(normed, w_in[1], preferred_element_type=jnp.float32)  11.9 us
  transfers between devices with their start and end apart: 10, of which 4 were waited for; matrix products, arithmetic and copies ran while one was open for 12% of the time, Pallas kernels for 0%

profile of v1, /device:TPU:0, one launch (start us, length us, event | category | flops | bytes accessed | tf_op | source)
XLA Modules:
  0.0 542.6 jit_solution(6490281593102442310)
XLA Ops:
  6.5 1.4 copy.59
  8.0 7.0 %reshape_squeeze.15 = bf16[4096,2,256]{2,1,0:T(2,128)(2,1)} reshape(bf16[1,4096,512]{2,1,0:T(8,128)(2,1)} %param.11) | data formatting | bytes 8388608 | tf_op jit(solution)/shard_map/reshape;squeeze | solution.py:83
  15.8 1.4 fusion.23
  17.8 12.0 %bitcast_reduce_fusion = (f32[2,3,256]{2,1,0:T(4,128)S(1)}, f32[2,4096,256,3]{2,1,3,0:T(8,128)}) fusion(pred[4096]{0:T(1024)(128)(4,1)S(1)} %add_compare_fusion, bf16[256,2,3,256]{0,3,2,1:T(8,128)(2,1)S(1)} %bitcast.64, bf16[4096,2,256,1]{2,1,0,3:T(2,128)(2,1)} %bitcast.62), kind=kOutput, calls=%fused_computation.1 | convolution fusion | flops 3240098304 | bytes 30156800 | tf_op jit(solution)/shard_map/ngrd,cgd->grnc/dot_general | solution.py:90
  30.1 2.6 pmax.7
  32.7 11.4 %fusion.1 = f32[2,3,256]{2,1,0:T(4,128)S(1)} fusion(f32[2,4096,256,3]{2,1,3,0:T(8,128)} %get-tuple-element.8, f32[2,3,256]{2,1,0:T(4,128)S(1)} %pmax.7, pred[4096]{0:T(1024)(128)(4,1)S(1)} %add_compare_fusion), kind=kLoop, calls=%fused_computation.4 | loop fusion | flops 25164288 | bytes 25182208 | tf_op jit(solution)/shard_map/reduce_sum | solution.py:109
  45.2 6.9 %reshape_squeeze.18 = bf16[4096,2,256]{2,1,0:T(2,128)(2,1)} reshape(bf16[1,4096,512]{2,1,0:T(8,128)(2,1)} %param.12) | data formatting | bytes 8388608 | tf_op jit(solution)/shard_map/reshape;squeeze | solution.py:84
  52.1 13.5 %fusion.3 = f32[2,3,256,256]{3,2,1,0:T(8,128)S(1)} fusion(f32[2,4096,256,3]{2,1,3,0:T(8,128)} %get-tuple-element.8, f32[2,3,256]{2,1,0:T(4,128)S(1)} %pmax.7, pred[4096]{0:T(1024)(128)(4,1)S(1)} %add_compare_fusion, bf16[4096,2,256,1]{2,1,0,3:T(2,128)(2,1)} %bitcast.63), kind=kOutput, calls=%fused_computation.6 | convolution fusion | flops 3246391296 | bytes 30943232 | tf_op jit(solution)/shard_map/grnc,cgd->ngrd/dot_general | solution.py:112
  65.7 1.7 reshape_squeeze.19
  67.3 2.5 add_bitcast_fusion
  69.9 1.5 pad_maximum_fusion
  71.3 5.3 copy.69
  76.6 8.1 %all-to-all-start = ((bf16[2,96,6144]{1,0,2:T(2,128)(2,1)}), bf16[2,96,6144]{1,0,2:T(2,128)(2,1)S(1)}, u32[]{:S(2)}, u32[]{:S(2)}) async-start(bf16[2,96,6144]{1,0,2:T(2,128)(2,1)} %copy.69), calls=%async_computation.1 | async-start | bytes 6291456 | tf_op jit(solution)/shard_map/all_to_all | solution.py:121
  86.1 2.2 multiply_reduce_fusion
  88.3 2.3 copy.68
  91.8 2.0 collective-permute-start
  93.8 10.6 %collective-permute-done = bf16[128,1536]{0,1:T(8,128)(2,1)} collective-permute-done((bf16[128,1536]{0,1:T(8,128)(2,1)S(1)}, bf16[128,1536]{0,1:T(8,128)(2,1)}, u32[]{:S(2)}, u32[]{:S(2)}) %collective-permute-start) | collective-permute-done | bytes 393248 | tf_op jit(solution)/shard_map/ppermute | solution.py:137
  104.4 2.2 maximum_select_fusion.5
  106.6 3.9 collective-permute-start.1
  110.5 27.6 %collective-permute-done.1 = bf16[256,1536]{0,1:T(8,128)(2,1)} collective-permute-done((bf16[256,1536]{0,1:T(8,128)(2,1)}, bf16[256,1536]{0,1:T(8,128)(2,1)}, u32[]{:S(2)}, u32[]{:S(2)}) %collective-permute-start.1) | collective-permute-done | bytes 786464 | tf_op jit(solution)/shard_map/ppermute | solution.py:137
  138.1 3.5 maximum_select_fusion.2
  141.5 5.7 %collective-permute-start.2 = (bf16[512,1536]{0,1:T(8,128)(2,1)}, bf16[512,1536]{0,1:T(8,128)(2,1)}, u32[]{:S(2)}, u32[]{:S(2)}) collective-permute-start(bf16[512,1536]{0,1:T(8,128)(2,1)} %maximum_select_fusion.2), channel_id=1, source_target_pairs={{0,8},{2,10},{4,12},{6,14},{8,0},{10,2},{12,4},{14,6},{16,24},{18,... | collective-permute-start | bytes 4718600 | tf_op jit(solution)/shard_map/ppermute | solution.py:137
  147.2 5.5 %copy.91 = bf16[2,96,16,384]{3,1,2,0:T(8,128)(2,1)} copy(bf16[2,96,16,384]{1,0,3,2:T(2,128)(2,1)S(1)} %bitcast.57) | data formatting | bytes 4718592 | tf_op jit(solution)/shard_map/all_to_all | solution.py:121
  152.8 28.6 %collective-permute-done.2 = bf16[512,1536]{0,1:T(8,128)(2,1)} collective-permute-done((bf16[512,1536]{0,1:T(8,128)(2,1)}, bf16[512,1536]{0,1:T(8,128)(2,1)}, u32[]{:S(2)}, u32[]{:S(2)}) %collective-permute-start.2) | collective-permute-done | bytes 1572896 | tf_op jit(solution)/shard_map/ppermute | solution.py:137
  181.4 4.1 maximum_select_fusion.1
  185.5 8.1 %collective-permute-start.3 = (bf16[1024,1536]{0,1:T(8,128)(2,1)S(1)}, bf16[1024,1536]{0,1:T(8,128)(2,1)}, u32[]{:S(2)}, u32[]{:S(2)}) collective-permute-start(bf16[1024,1536]{0,1:T(8,128)(2,1)S(1)} %maximum_select_fusion.1), channel_id=1, source_target_pairs={{0,16},{2,18},{4,20},{6,22},{8,24},{10,26},{12,28},{14,30},{16,0},... | collective-permute-start | bytes 9437192 | tf_op jit(solution)/shard_map/ppermute | solution.py:137
  193.6 1.4 copy.109
  195.0 159.3 %all_to_all.37 = bf16[16,384,96]{1,2,0:T(8,128)(2,1)} all-to-all(bf16[16,384,96]{1,2,0:T(8,128)(2,1)S(1)} %bitcast.61), channel_id=1, replica_groups=mesh['req'=16,'mlp'=2] {'req'}, dimensions={0} | all-to-all | bytes 2359296 | tf_op jit(solution)/shard_map/all_to_all | solution.py:123
  354.4 11.9 %fusion.10 = f32[2048,768]{1,0:T(8,128)} fusion(bf16[2,1536,768]{2,1,0:T(8,128)(2,1)} %all-gather.3.cloned.1.call-done, bf16[1024,1536]{0,1:T(8,128)(2,1)} %collective-permute-done.3, bf16[1024,1536]{0,1:T(8,128)(2,1)S(1)} %maximum_select_fusion.1, pred[]{:T(512)S(6)} %eq.28), kind=kOutput, calls=%fused_computation.17 | convolution fusion | flops 4860149760 | bytes 14942209 | tf_op jit(solution)/shard_map/dot_general | solution.py:143
  366.3 21.2 %convolution_convert_fusion = bf16[2048,1536]{1,0:T(8,128)(2,1)} fusion(bf16[768,1536]{0,1:T(8,128)(2,1)} %all-gather.5.cloned.1.call-done, f32[2048,768]{1,0:T(8,128)} %fusion.10, bf16[2,1536,768]{2,1,0:T(8,128)(2,1)} %all-gather.3.cloned.1.call-done, bf16[1024,1536]{0,1:T(8,128)(2,1)} %collective-permute-done.3, ...), kind=kOutput, calls=%fused_computation.8 | convolution fusion | flops 9704570880 | bytes 23592960 | tf_op jit(solution)/shard_map/dot_general | solution.py:145
  388.9 145.4 %reduce-scatter.8.cloned.1.call-done = bf16[128,1536]{1,0:T(8,128)(2,1)} async-done(((bf16[2048,1536]{1,0:T(8,128)(2,1)}), bf16[128,1536]{1,0:T(8,128)(2,1)}) %reduce-scatter.8.cloned.1.call-update) | async-done | bytes 393232 | tf_op jit(solution)/shard_map/reduce_scatter | solution.py:146
  534.3 1.8 fusion.18
  (42 shorter events, 6.8 us)
Async XLA Ops:
  6.5 78.5 %reduce-scatter.10.cloned.1.call-start = ((), (), s32[]{:S(2)}) async-start(), calls=%async_computation.9 | async-start | bytes 196608
  7.9 7.0 %copy-start.2 = (bf16[1,128,512]{2,1,0:T(8,128)(2,1)S(1)}, bf16[1,128,512]{2,1,0:T(8,128)(2,1)}, u32[]{:S(2)}) copy-start(bf16[1,128,512]{2,1,0:T(8,128)(2,1)} %param.13) | copy-start | bytes 393220
  8.0 7.2 %copy-start.3 = (s32[16]{0:T(128)S(1)}, s32[16]{0:T(128)}, u32[]{:S(2)}) copy-start(s32[16]{0:T(128)} %param.16) | copy-start | bytes 196
  8.0 7.8 %copy-start.4 = (s32[16]{0:T(128)S(1)}, s32[16]{0:T(128)}, u32[]{:S(2)}) copy-start(s32[16]{0:T(128)} %param.15) | copy-start | bytes 196
  45.2 40.9 %reduce-scatter.6.cloned.1.call-start = ((), (), s32[]{:S(2)}) async-start(), calls=%async_computation.5 | async-start | bytes 2359296 | tf_op jit(solution)/shard_map/reduce_scatter | solution.py:126
  65.6 4.2 copy-start.1
  76.6 70.6 %all-to-all-start = ((bf16[2,96,6144]{1,0,2:T(2,128)(2,1)}), bf16[2,96,6144]{1,0,2:T(2,128)(2,1)S(1)}, u32[]{:S(2)}, u32[]{:S(2)}) async-start(bf16[2,96,6144]{1,0,2:T(2,128)(2,1)} %copy.69), calls=%async_computation.1 | async-start | bytes 6291456 | tf_op jit(solution)/shard_map/all_to_all | solution.py:121
  84.8 269.6 %all-gather.3.cloned.1.call-start = ((), (), s32[]{:S(2)}) async-start(), calls=%async_computation.6 | async-start | bytes 7077888 | tf_op jit(solution)/shard_map/all_gather | solution.py:122
  91.8 12.6 %collective-permute-start = (bf16[128,1536]{0,1:T(8,128)(2,1)S(1)}, bf16[128,1536]{0,1:T(8,128)(2,1)}, u32[]{:S(2)}, u32[]{:S(2)}) collective-permute-start(bf16[128,1536]{0,1:T(8,128)(2,1)S(1)} %multiply_convert_fusion.2), channel_id=1, source_target_pairs={{0,2},{2,0},{4,6},{6,4},{8,10},{10,8},{12,14},{14,12},{16,18},{18,... | collective-permute-start | bytes 1179656 | tf_op jit(solution)/shard_map/ppermute | solution.py:137
  106.6 31.5 %collective-permute-start.1 = (bf16[256,1536]{0,1:T(8,128)(2,1)}, bf16[256,1536]{0,1:T(8,128)(2,1)}, u32[]{:S(2)}, u32[]{:S(2)}) collective-permute-start(bf16[256,1536]{0,1:T(8,128)(2,1)} %maximum_select_fusion.5), channel_id=1, source_target_pairs={{0,4},{2,6},{4,0},{6,2},{8,12},{10,14},{12,8},{14,10},{16,20},{18,... | collective-permute-start | bytes 2359304 | tf_op jit(solution)/shard_map/ppermute | solution.py:137
  141.5 39.9 %collective-permute-start.2 = (bf16[512,1536]{0,1:T(8,128)(2,1)}, bf16[512,1536]{0,1:T(8,128)(2,1)}, u32[]{:S(2)}, u32[]{:S(2)}) collective-permute-start(bf16[512,1536]{0,1:T(8,128)(2,1)} %maximum_select_fusion.2), channel_id=1, source_target_pairs={{0,8},{2,10},{4,12},{6,14},{8,0},{10,2},{12,4},{14,6},{16,24},{18,... | collective-permute-start | bytes 4718600 | tf_op jit(solution)/shard_map/ppermute | solution.py:137
  152.7 213.5 %all-gather.5.cloned.1.call-start = ((), (), s32[]{:S(2)}) async-start(), calls=%async_computation.7 | async-start | bytes 3538944 | tf_op jit(solution)/shard_map/all_gather | solution.py:124
  185.5 168.8 %collective-permute-start.3 = (bf16[1024,1536]{0,1:T(8,128)(2,1)S(1)}, bf16[1024,1536]{0,1:T(8,128)(2,1)}, u32[]{:S(2)}, u32[]{:S(2)}) collective-permute-start(bf16[1024,1536]{0,1:T(8,128)(2,1)S(1)} %maximum_select_fusion.1), channel_id=1, source_target_pairs={{0,16},{2,18},{4,20},{6,22},{8,24},{10,26},{12,28},{14,30},{16,0},... | collective-permute-start | bytes 9437192 | tf_op jit(solution)/shard_map/ppermute | solution.py:137
  354.3 180.0 %reduce-scatter.8.cloned.1.call-start = ((), (), s32[]{:S(2)}) async-start(), calls=%async_computation.8 | async-start | bytes 6684672 | tf_op jit(solution)/shard_map/reduce_scatter | solution.py:146
  387.5 1.1 copy-start
Sparse Core Ops, SparseCore 0:
  45.3 10.0 reduce-scatter.9
  70.0 11.5 reduce-scatter.5
  152.8 23.2 all-gather.2
  354.4 11.7 all-gather.4
  387.6 146.6 reduce-scatter.7
